TPU v7x, 32 devices: a whole 2x2x4 slice. The times are simulated.
32 devices in a mesh: dap: 8 (over z, x), head: 4 (over y, core).
Axes of the slice: x: 2, y: 2, z: 4, core: 2. Of those that a mesh axis runs over, the one named last changes fastest.
Arguments:
- multiple_aligned_family: bfloat16 [128, 128, 256], P('dap')
- homolog_present_flags: int32 [128], replicated, may hold values from 0 to 1, as said below
- amino_present_flags: int32 [128], replicated, may hold values 0 or 1
- focus_layernorm_scaling: float32 [256], replicated, may hold values from 0.5 to 1.5
- focus_layernorm_offset: float32 [256], replicated, may hold values from -1.8 to 1.8
- combined_focus_matrices: bfloat16 [256, 4, 256], P(None, None, 'head')
- sigmoid_switch_offset: float32 [256], P('head'), may hold values from -4 to 4
- focus_final_matrix: bfloat16 [256, 256], P('head'), may hold values from -0.375 to 0.375
- focus_final_offset: float32 [256], replicated, may hold values from -3 to 3
- tensor_layernorm_scaling: float32 [256], replicated, may hold values from 0.5 to 1.5
- tensor_layernorm_offset: float32 [256], replicated, may hold values from -1.8 to 1.8
- tensor_product_factors: bfloat16 [256, 2, 32], replicated, may hold values from -0.375 to 0.375
- tensor_final_matrix: float32 [1024, 128], replicated, may hold values from -0.1875 to 0.1875
- tensor_final_offset: float32 [128], replicated, may hold values from -4 to 4
Outputs:
- alignment_output: bfloat16 [128, 128, 256], P(('dap', 'head'))
- pair_mean_update: float32 [128, 128, 128], P('dap', 'head')
Inputs may be any that keep to these rules, and one draw needn't show every extreme that they name: homolog_present_flags[0] is always 1.
All inputs are finite; a program needn't handle non-finite values.
Results may differ from a plain program's by a relative error of at most 0.005.
Values may be sent and summed in bfloat16 or wider, within the bound.
A program may use at most 256 MiB of HBM per device.

v0:
```python
import jax
import jax.numpy as jnp
from jax import lax
from jax.sharding import PartitionSpec as P

DH = 32
CO = 32


def layer_norm(value, gain, bias):
    mean = jnp.mean(value, -1, keepdims=True)
    centred = value - mean
    spread = jnp.mean(centred * centred, -1, keepdims=True)
    return centred * lax.rsqrt(spread + 1e-05) * gain + bias


def attend_column(query, keys, values, gate, keep):
    scores = jnp.einsum("shd,thd->hst", query, keys, preferred_element_type=jnp.float32)
    scores = jnp.where(keep[None, None, :], scores, jnp.float32(-1000000000.0))
    top = jnp.max(scores, -1, keepdims=True)
    weights = jnp.exp(scores - top)
    probs = (weights / jnp.sum(weights, -1, keepdims=True)).astype(jnp.bfloat16)
    mixed = jnp.einsum("hst,thd->shd", probs, values, preferred_element_type=jnp.float32)
    return (mixed * gate).astype(jnp.bfloat16)


def per_device(
    multiple_aligned_family,
    homolog_present_flags,
    amino_present_flags,
    focus_layernorm_scaling,
    focus_layernorm_offset,
    combined_focus_matrices,
    sigmoid_switch_offset,
    focus_final_matrix,
    focus_final_offset,
    tensor_layernorm_scaling,
    tensor_layernorm_offset,
    tensor_product_factors,
    tensor_final_matrix,
    tensor_final_offset,
):
    parallel_devices = lax.axis_size("dap")
    n_head = lax.axis_size("head")
    head_id = lax.axis_index("head")
    dap_id = lax.axis_index("dap")
    homolog_shard_number, amino_total, feature_dimension = multiple_aligned_family.shape
    total_seqs = homolog_present_flags.shape[0]
    residue_device_count = amino_total // parallel_devices
    local_heads = sigmoid_switch_offset.shape[0] // DH
    keep = homolog_present_flags > 0
    weights_in = combined_focus_matrices.reshape(feature_dimension, 4 * local_heads * DH)
    gate_shift = sigmoid_switch_offset.reshape(local_heads, DH)
    bundled_focus_units = multiple_aligned_family.reshape(
        homolog_shard_number, parallel_devices, residue_device_count, feature_dimension
    )
    received = lax.all_to_all(bundled_focus_units, "dap", split_axis=1, concat_axis=0, tiled=True)
    block = received[:, 0]
    count = block.shape[1]
    normed = layer_norm(
        block.astype(jnp.float32), focus_layernorm_scaling, focus_layernorm_offset
    ).astype(jnp.bfloat16)
    projected = jnp.dot(
        normed.reshape(total_seqs * count, feature_dimension),
        weights_in,
        preferred_element_type=jnp.float32,
    )
    projected = projected.reshape(total_seqs, count, 4, local_heads, DH)
    query = jnp.moveaxis((projected[:, :, 0] * DH ** (-0.5)).astype(jnp.bfloat16), 1, 0)
    keys = jnp.moveaxis(projected[:, :, 1].astype(jnp.bfloat16), 1, 0)
    values = jnp.moveaxis(projected[:, :, 2].astype(jnp.bfloat16), 1, 0)
    gate = jnp.moveaxis(jax.nn.sigmoid(projected[:, :, 3] + gate_shift), 1, 0)

    def single(operands):
        return attend_column(operands[0], operands[1], operands[2], operands[3], keep)

    attended = lax.map(single, (query, keys, values, gate))
    attended = jnp.moveaxis(attended, 0, 1).reshape(total_seqs * count, local_heads * DH)
    partial_value = jnp.dot(attended, focus_final_matrix, preferred_element_type=jnp.float32)
    partial_value, columns = (
        partial_value.reshape(total_seqs, 1, count, feature_dimension),
        received,
    )
    group = homolog_shard_number // n_head
    columns = columns.reshape(
        parallel_devices, n_head, group, residue_device_count, feature_dimension
    )
    partial_value = partial_value.reshape(
        parallel_devices, n_head, group, residue_device_count, feature_dimension
    )
    summed = lax.psum(partial_value.astype(jnp.bfloat16), "head").astype(jnp.float32)
    summed_mine = lax.dynamic_index_in_dim(summed, head_id, 1, keepdims=True)
    own = lax.dynamic_index_in_dim(columns, head_id, 1, keepdims=True)
    mine = (own.astype(jnp.float32) + summed_mine + focus_final_offset).astype(jnp.bfloat16)
    alignment_rows = lax.all_to_all(
        mine.reshape(parallel_devices * group, residue_device_count, feature_dimension),
        "dap",
        split_axis=0,
        concat_axis=1,
        tiled=True,
    )
    seq_keep = homolog_present_flags.astype(jnp.float32).reshape(parallel_devices, n_head, group)
    row_keep = lax.dynamic_slice_in_dim(
        amino_present_flags, dap_id * residue_device_count, residue_device_count
    ).astype(jnp.float32)
    stack = mine.reshape(parallel_devices * group, residue_device_count, feature_dimension)
    mask_seq = lax.dynamic_index_in_dim(seq_keep, head_id, 1, keepdims=False).reshape(
        parallel_devices * group
    )
    left_weight = tensor_product_factors[:, 0]
    right_weight = tensor_product_factors[:, 1]
    used = stack.shape[0]
    opm_normed = layer_norm(
        stack.astype(jnp.float32), tensor_layernorm_scaling, tensor_layernorm_offset
    ).astype(jnp.bfloat16)
    flat = opm_normed.reshape(used * residue_device_count, feature_dimension)
    keep_rs = mask_seq[:, None, None] * row_keep[None, :, None]
    left = (
        jnp.dot(flat, left_weight, preferred_element_type=jnp.float32).reshape(
            used, residue_device_count, -1
        )
        * keep_rs
    ).astype(jnp.bfloat16)
    right = (
        jnp.dot(flat, right_weight, preferred_element_type=jnp.float32).reshape(
            used, residue_device_count, CO
        )
        * keep_rs
    ).astype(jnp.bfloat16)
    piece = lax.all_gather(right, "dap", axis=1, tiled=True)
    outer = lax.dot_general(
        left, piece, (((0,), (0,)), ((), ())), preferred_element_type=jnp.float32
    )
    outer = outer.transpose(0, 2, 1, 3).reshape(residue_device_count, piece.shape[1], -1)
    partial_pair = jnp.dot(
        outer,
        tensor_final_matrix,
        precision=lax.Precision.HIGHEST,
        preferred_element_type=jnp.float32,
    )
    pair = lax.psum_scatter(partial_pair, "head", scatter_dimension=1, tiled=True)
    col_width = amino_total // n_head
    col_keep = lax.dynamic_slice_in_dim(amino_present_flags, head_id * col_width, col_width).astype(
        jnp.float32
    )
    count = jnp.sum(homolog_present_flags).astype(jnp.float32)
    norm = jnp.maximum(count * row_keep[:, None] * col_keep[None, :], 1.0)
    pair_mean_update = (pair + tensor_final_offset) / norm[:, :, None]
    return (alignment_rows, pair_mean_update)


def solution(mesh):
    return jax.shard_map(
        per_device,
        mesh=mesh,
        in_specs=(
            P("dap", None, None),
            P(),
            P(),
            P(),
            P(),
            P(None, None, "head"),
            P("head"),
            P("head", None),
            P(),
            P(),
            P(),
            P(),
            P(),
            P(),
        ),
        out_specs=(P(("dap", "head"), None, None), P("dap", "head", None)),
        check_vma=False,
    )
```

profile of v0, /device:TPU:0, one launch (start us, length us, event | category | flops | bytes accessed | tf_op | source)
XLA Modules:
  0.0 189.5 jit_solution(11915135432507252343)
XLA Ops:
  7.2 2.4 %copy.23 = bf16[16,8,16,256]{3,2,0,1:T(8,128)(2,1)} copy(bf16[16,8,16,256]{3,2,1,0:T(8,128)(2,1)} %bitcast.152) | data formatting | bytes 2097152 | tf_op jit(solution)/shard_map/reshape | solution.py:54
  9.6 7.4 %all-to-all-start = ((bf16[16,8,16,256]{3,2,0,1:T(8,128)(2,1)}), bf16[16,8,16,256]{3,2,0,1:T(8,128)(2,1)S(1)}, u32[]{:S(2)}, u32[]{:S(2)}) async-start(bf16[16,8,16,256]{3,2,0,1:T(8,128)(2,1)} %copy.23), calls=%async_computation | async-start | bytes 2097152 | tf_op jit(solution)/shard_map/all_to_all | solution.py:57
  17.1 25.6 %all-to-all-done = bf16[16,8,16,256]{3,2,0,1:T(8,128)(2,1)S(1)} async-done(((bf16[16,8,16,256]{3,2,0,1:T(8,128)(2,1)}), bf16[16,8,16,256]{3,2,0,1:T(8,128)(2,1)S(1)}, u32[]{:S(2)}, u32[]{:S(2)}) %all-to-all-start) | async-done | bytes 1048608 | tf_op jit(solution)/shard_map/all_to_all | solution.py:57
  43.1 0.7 fusion.43
  43.8 0.7 fusion.46
  44.9 0.5 fusion.79
  45.8 10.6 %while.10 = (s32[]{:T(128)}, bf16[16,128,2,32]{1,3,2,0:T(8,128)(2,1)S(1)}, bf16[16,128,2,32]{1,3,2,0:T(8,128)(2,1)S(1)}, pred[128]{0:T(512)(128)(4,1)S(1)}, bf16...) while((s32[]{:T(128)}, ...), condition=%wide.region_5.6_spmd, body=%wide.region_2.5_spmd.sunk | while | flops 6537728 | bytes 137301 | solution.py:77
  46.0 0.4 fusion.99
  47.4 0.4 fusion.99
  48.0 0.4 fusion.99
  50.0 0.4 fusion.99
  50.7 0.4 fusion.99
  52.0 0.4 fusion.99
  52.7 0.4 fusion.99
  54.0 0.4 fusion.99
  56.4 0.9 copy.25
  57.3 0.5 dot_general.33
  57.9 1.4 convolution_convert_fusion
  59.4 0.6 fusion.78
  61.1 33.8 %all-reduce.2.cloned.1.call-done = bf16[8,4,4,16,256]{4,3,2,1,0:T(8,128)(2,1)} async-done(((bf16[8,4,4,16,256]{4,3,2,1,0:T(8,128)(2,1)}), bf16[8,4,4,16,256]{4,3,2,1,0:T(8,128)(2,1)}) %all-reduce.2.cloned.1.call-update) | async-done | bytes 1048592 | tf_op jit(solution)/shard_map/psum | solution.py:91
  94.8 1.7 convert_reduce_fusion.1
  96.6 1.2 fusion.50
  97.9 1.2 fusion.53
  99.9 33.2 %all_gather.3 = bf16[32,128,32]{0,1,2:T(8,128)(2,1)S(1)} all-gather(bf16[32,16,32]{0,1,2:T(8,128)(2,1)S(1)} %get-tuple-element.61), channel_id=1, replica_groups=mesh['dap'=8,'head'=4] {'dap'}, dimensions={1}, use_global_device_ids=true | all-gather | bytes 294912 | tf_op jit(solution)/shard_map/all_gather | solution.py:130
  133.1 1.3 convolution_bitcast_fusion.1
  134.3 6.5 %copy.28 = f32[16,128,32,32]{1,3,2,0:T(8,128)S(1)} copy(f32[16,128,32,32]{1,2,3,0:T(8,128)S(1)} %convolution_bitcast_fusion.1) | data formatting | bytes 16777216 | tf_op jit(solution)/shard_map/transpose | solution.py:134
  140.8 14.9 %fusion.61 = f32[16,128,128]{2,1,0:T(8,128)} fusion(f32[16,128,1024]{1,2,0:T(8,128)S(1)} %bitcast.147, f32[1024,128]{1,0:T(8,128)S(1)} %copy-done), kind=kOutput, calls=%fused_computation.52 | convolution fusion | flops 3221225472 | bytes 9961472 | tf_op jit(solution)/shard_map/dot_general | solution.py:135
  155.7 5.4 %all-to-all-start.1 = ((bf16[32,16,256]{2,1,0:T(8,128)(2,1)}), bf16[32,16,256]{2,1,0:T(8,128)(2,1)S(1)}, u32[]{:S(2)}, u32[]{:S(2)}) async-start(bf16[32,16,256]{2,1,0:T(8,128)(2,1)} %bitcast.29), calls=%async_computation.1 | async-start | bytes 524288 | tf_op jit(solution)/shard_map/all_to_all | solution.py:95
  161.2 8.1 %all-to-all-done.1 = bf16[32,16,256]{2,1,0:T(8,128)(2,1)S(1)} async-done(((bf16[32,16,256]{2,1,0:T(8,128)(2,1)}), bf16[32,16,256]{2,1,0:T(8,128)(2,1)S(1)}, u32[]{:S(2)}, u32[]{:S(2)}) %all-to-all-start.1) | async-done | bytes 262176 | tf_op jit(solution)/shard_map/all_to_all | solution.py:95
  169.3 0.7 copy.26
  170.0 10.8 %reduce-scatter.2.cloned.1.call-done = f32[16,32,128]{2,1,0:T(8,128)} async-done(((f32[16,128,128]{2,1,0:T(8,128)}), f32[16,32,128]{2,1,0:T(8,128)}) %reduce-scatter.2.cloned.1.call-update) | async-done | bytes 262160 | tf_op jit(solution)/shard_map/reduce_scatter | solution.py:141
  180.8 1.8 add_divide_fusion
  (78 shorter events, 10.2 us)
Async XLA Ops:
  7.2 133.6 %copy-start = (f32[1024,128]{1,0:T(8,128)S(1)}, f32[1024,128]{1,0:T(8,128)}, u32[]{:S(2)}) copy-start(f32[1024,128]{1,0:T(8,128)} %param.28) | copy-start | bytes 1572868
  7.2 9.9 %copy-start.11 = (f32[64]{0:T(128)S(1)}, f32[64]{0:T(128)}, u32[]{:S(2)}) copy-start(f32[64]{0:T(128)} %param.22) | copy-start | bytes 772
  7.2 9.9 %copy-start.12 = (s32[128]{0:T(128)S(1)}, s32[128]{0:T(128)}, u32[]{:S(2)}) copy-start(s32[128]{0:T(128)} %param.17) | copy-start | bytes 1540
  9.6 34.2 %copy-start.4 = (f32[256]{0:T(256)S(1)}, f32[256]{0:T(256)}, u32[]{:S(2)}) copy-start(f32[256]{0:T(256)} %param.20) | copy-start | bytes 3076
  9.6 34.2 %copy-start.5 = (f32[256]{0:T(256)S(1)}, f32[256]{0:T(256)}, u32[]{:S(2)}) copy-start(f32[256]{0:T(256)} %param.19) | copy-start | bytes 3076
  9.6 33.2 %all-to-all-start = ((bf16[16,8,16,256]{3,2,0,1:T(8,128)(2,1)}), bf16[16,8,16,256]{3,2,0,1:T(8,128)(2,1)S(1)}, u32[]{:S(2)}, u32[]{:S(2)}) async-start(bf16[16,8,16,256]{3,2,0,1:T(8,128)(2,1)} %copy.23), calls=%async_computation | async-start | bytes 2097152 | tf_op jit(solution)/shard_map/all_to_all | solution.py:57
  17.0 77.9 %all-reduce.2.cloned.1.call-start = ((), (), s32[]{:S(2)}) async-start(), calls=%async_computation.3 | async-start | bytes 2097152 | tf_op jit(solution)/shard_map/psum | solution.py:91
  43.8 1.1 copy-start.1
  56.4 1.5 copy-start.2
  57.3 3.6 %copy-start.10 = (s32[128]{0:T(128)S(1)}, s32[128]{0:T(128)}, u32[]{:S(2)}) copy-start(s32[128]{0:T(128)} %param.18) | copy-start | bytes 1540
  57.3 37.5 %copy-start.6 = (f32[256]{0:T(256)S(1)}, f32[256]{0:T(256)}, u32[]{:S(2)}) copy-start(f32[256]{0:T(256)} %param.24) | copy-start | bytes 3076
  57.8 40.0 %copy-start.7 = (f32[256]{0:T(256)S(1)}, f32[256]{0:T(256)}, u32[]{:S(2)}) copy-start(f32[256]{0:T(256)} %param.26) | copy-start | bytes 3076
  57.9 40.0 %copy-start.8 = (f32[256]{0:T(256)S(1)}, f32[256]{0:T(256)}, u32[]{:S(2)}) copy-start(f32[256]{0:T(256)} %param.25) | copy-start | bytes 3076
  57.9 41.2 %copy-start.3 = (bf16[256,2,32]{0,2,1:T(8,128)(2,1)S(1)}, bf16[256,2,32]{0,2,1:T(8,128)(2,1)}, u32[]{:S(2)}) copy-start(bf16[256,2,32]{0,2,1:T(8,128)(2,1)} %param.27) | copy-start | bytes 98308
  59.3 121.5 %reduce-scatter.2.cloned.1.call-start = ((), (), s32[]{:S(2)}) async-start(), calls=%async_computation.4 | async-start | bytes 1310720 | tf_op jit(solution)/shard_map/reduce_scatter | solution.py:141
  155.7 25.1 %copy-start.9 = (f32[128]{0:T(128)S(1)}, f32[128]{0:T(128)}, u32[]{:S(2)}) copy-start(f32[128]{0:T(128)} %param.29) | copy-start | bytes 1540
  155.7 13.6 %all-to-all-start.1 = ((bf16[32,16,256]{2,1,0:T(8,128)(2,1)}), bf16[32,16,256]{2,1,0:T(8,128)(2,1)S(1)}, u32[]{:S(2)}, u32[]{:S(2)}) async-start(bf16[32,16,256]{2,1,0:T(8,128)(2,1)} %bitcast.29), calls=%async_computation.1 | async-start | bytes 524288 | tf_op jit(solution)/shard_map/all_to_all | solution.py:95
Sparse Core Ops, SparseCore 0:
  59.5 35.3 all-reduce.1
  155.9 24.9 reduce-scatter.1
where the time goes:
time: 190 us; the launch traced here: 189 us
  waiting for transfers between devices  78.3 us (41%)
  blocking collectives  33.2 us (17%)
  matrix products  29 us (15%)
  between operations  15.1 us (8%)
  starting transfers between devices  12.8 us (7%)
  local copies, waits for them, and re-layouts  12.1 us (6%)
  other arithmetic  8.95 us (5%)
    psum x1, waiting for transfers between devices, per_device(): lax.psum(partial_value.astype(jnp.bfloat16), 'head').astype(jnp.float32)  33.8 us
    all_gather x1, blocking collectives, per_device(): piece = lax.all_gather(right, 'dap', axis=1, tiled=True)  33.2 us
    all_to_all x1, waiting for transfers between devices, per_device(): lax.all_to_all(bundled_focus_units, 'dap', split_axis=1, concat_axis=0, t...  25.6 us
    dot_general x1, matrix products, per_device(): jnp.dot(outer, tensor_final_matrix, precision=lax.Precision.HIGHEST, pref...  14.9 us
    reduce_scatter x1, waiting for transfers between devices, per_device(): lax.psum_scatter(partial_pair, 'head', scatter_dimension=1, tiled=True)  10.8 us
    all_to_all x1, waiting for transfers between devices, per_device(): lax.all_to_all(mine.reshape(parallel_devices * group, residue_device_coun...  8.07 us
    all_to_all x1, starting transfers between devices, per_device(): lax.all_to_all(bundled_focus_units, 'dap', split_axis=1, concat_axis=0, t...  7.41 us
    transpose x1, local copies, waits for them, and re-layouts, per_device(): outer.transpose(0, 2, 1, 3)  6.49 us
  transfers between devices with their start and end apart: 4, of which 4 were waited for; matrix products, arithmetic and copies ran while one was open for 1% of the time, Pallas kernels for 0%

commit v1 on v0

--- a/solution.py
+++ b/solution.py
@@ -2,6 +2,7 @@
 import jax.numpy as jnp
 from jax import lax
 from jax.sharding import PartitionSpec as P
+from jax.lax import all_gather
 
 DH = 32
 CO = 32
@@ -127,7 +128,7 @@
         )
         * keep_rs
     ).astype(jnp.bfloat16)
-    piece = lax.all_gather(right, "dap", axis=1, tiled=True)
+    piece = jnp.concatenate(all_gather(right, "dap"), axis=1)
     outer = lax.dot_general(
         left, piece, (((0,), (0,)), ((), ())), preferred_element_type=jnp.float32
     )

time: 190 us -> 190 us (level)
  no operation moved by 1% of the time
where the time goes in v1:
time: 190 us
  waiting for transfers between devices  78.2 us (41%)
  blocking collectives  33.3 us (18%)
  matrix products  29.1 us (15%)
  between operations  15 us (8%)
  starting transfers between devices  12.7 us (7%)
  local copies, waits for them, and re-layouts  12.6 us (7%)
  other arithmetic  8.91 us (5%)
    psum x1, waiting for transfers between devices, per_device(): lax.psum(partial_value.astype(jnp.bfloat16), 'head').astype(jnp.float32)  33.8 us
    all_gather x1, blocking collectives, per_device(): piece = jnp.concatenate(all_gather(right, 'dap'), axis=1)  33.3 us
    all_to_all x1, waiting for transfers between devices, per_device(): lax.all_to_all(bundled_focus_units, 'dap', split_axis=1, concat_axis=0, t...  25.6 us
    dot_general x1, matrix products, per_device(): jnp.dot(outer, tensor_final_matrix, precision=lax.Precision.HIGHEST, pref...  14.9 us
    reduce_scatter x1, waiting for transfers between devices, per_device(): lax.psum_scatter(partial_pair, 'head', scatter_dimension=1, tiled=True)  10.8 us
    all_to_all x1, waiting for transfers between devices, per_device(): lax.all_to_all(mine.reshape(parallel_devices * group, residue_device_coun...  8.07 us
    all_to_all x1, starting transfers between devices, per_device(): lax.all_to_all(bundled_focus_units, 'dap', split_axis=1, concat_axis=0, t...  7.41 us
    transpose x1, local copies, waits for them, and re-layouts, per_device(): outer.transpose(0, 2, 1, 3)  6.49 us
  transfers between devices with their start and end apart: 4, of which 4 were waited for; matrix products, arithmetic and copies ran while one was open for 1% of the time, Pallas kernels for 0%

profile of v1, /device:TPU:0, one launch (start us, length us, event | category | flops | bytes accessed | tf_op | source)
XLA Modules:
  0.0 189.9 jit_solution(5964433869791180840)
XLA Ops:
  7.2 2.4 %copy.34 = bf16[16,8,16,256]{3,2,0,1:T(8,128)(2,1)} copy(bf16[16,8,16,256]{3,2,1,0:T(8,128)(2,1)} %bitcast.158) | data formatting | bytes 2097152 | tf_op jit(solution)/shard_map/reshape | solution.py:55
  9.6 7.4 %all-to-all-start = ((bf16[16,8,16,256]{3,2,0,1:T(8,128)(2,1)}), bf16[16,8,16,256]{3,2,0,1:T(8,128)(2,1)S(1)}, u32[]{:S(2)}, u32[]{:S(2)}) async-start(bf16[16,8,16,256]{3,2,0,1:T(8,128)(2,1)} %copy.34), calls=%async_computation | async-start | bytes 2097152 | tf_op jit(solution)/shard_map/all_to_all | solution.py:58
  17.1 25.6 %all-to-all-done = bf16[16,8,16,256]{3,2,0,1:T(8,128)(2,1)S(1)} async-done(((bf16[16,8,16,256]{3,2,0,1:T(8,128)(2,1)}), bf16[16,8,16,256]{3,2,0,1:T(8,128)(2,1)S(1)}, u32[]{:S(2)}, u32[]{:S(2)}) %all-to-all-start) | async-done | bytes 1048608 | tf_op jit(solution)/shard_map/all_to_all | solution.py:58
  43.1 0.7 fusion.43
  43.8 0.7 fusion.46
  44.9 0.5 fusion.79
  45.8 10.6 %while.10 = (s32[]{:T(128)}, bf16[16,128,2,32]{1,3,2,0:T(8,128)(2,1)S(1)}, bf16[16,128,2,32]{1,3,2,0:T(8,128)(2,1)S(1)}, pred[128]{0:T(512)(128)(4,1)S(1)}, bf16...) while((s32[]{:T(128)}, ...), condition=%wide.region_5.6_spmd, body=%wide.region_2.5_spmd.sunk | while | flops 6537728 | bytes 137301 | solution.py:78
  46.0 0.4 fusion.99
  47.4 0.4 fusion.99
  48.0 0.4 fusion.99
  50.0 0.4 fusion.99
  50.7 0.4 fusion.99
  52.0 0.4 fusion.99
  52.7 0.4 fusion.99
  56.4 0.9 copy.36
  57.3 0.5 dot_general.33
  57.9 1.4 convolution_convert_fusion
  59.4 0.6 fusion.78
  61.1 33.8 %all-reduce.2.cloned.1.call-done = bf16[8,4,4,16,256]{4,3,2,1,0:T(8,128)(2,1)} async-done(((bf16[8,4,4,16,256]{4,3,2,1,0:T(8,128)(2,1)}), bf16[8,4,4,16,256]{4,3,2,1,0:T(8,128)(2,1)}) %all-reduce.2.cloned.1.call-update) | async-done | bytes 1048592 | tf_op jit(solution)/shard_map/psum | solution.py:92
  94.8 1.7 convert_reduce_fusion.1
  96.6 1.2 fusion.52
  97.9 1.2 fusion.55
  99.5 33.3 %all-gather = bf16[256,16,32]{2,1,0:T(8,128)(2,1)S(1)} all-gather(bf16[32,16,32]{2,1,0:T(8,128)(2,1)S(1)} %fusion.48), channel_id=2, replica_groups=mesh['dap'=8,'head'=4] {'dap'}, dimensions={0}, use_global_device_ids=true | all-gather | bytes 294912 | tf_op jit(solution)/shard_map/all_gather | solution.py:131
  133.1 0.5 copy.40
  133.7 1.3 convolution_bitcast_fusion.1
  134.9 6.5 %copy.41 = f32[16,128,32,32]{1,3,2,0:T(8,128)S(1)} copy(f32[16,128,32,32]{1,2,3,0:T(8,128)S(1)} %convolution_bitcast_fusion.1) | data formatting | bytes 16777216 | tf_op jit(solution)/shard_map/transpose | solution.py:135
  141.4 14.9 %fusion.63 = f32[16,128,128]{2,1,0:T(8,128)} fusion(f32[16,128,1024]{1,2,0:T(8,128)S(1)} %bitcast.151, f32[1024,128]{1,0:T(8,128)S(1)} %copy-done), kind=kOutput, calls=%fused_computation.56 | convolution fusion | flops 3221225472 | bytes 9961472 | tf_op jit(solution)/shard_map/dot_general | solution.py:136
  156.4 5.2 %all-to-all-start.1 = ((bf16[32,16,256]{2,1,0:T(8,128)(2,1)}), bf16[32,16,256]{2,1,0:T(8,128)(2,1)S(1)}, u32[]{:S(2)}, u32[]{:S(2)}) async-start(bf16[32,16,256]{2,1,0:T(8,128)(2,1)} %bitcast.29), calls=%async_computation.1 | async-start | bytes 524288 | tf_op jit(solution)/shard_map/all_to_all | solution.py:96
  161.7 8.1 %all-to-all-done.1 = bf16[32,16,256]{2,1,0:T(8,128)(2,1)S(1)} async-done(((bf16[32,16,256]{2,1,0:T(8,128)(2,1)}), bf16[32,16,256]{2,1,0:T(8,128)(2,1)S(1)}, u32[]{:S(2)}, u32[]{:S(2)}) %all-to-all-start.1) | async-done | bytes 262176 | tf_op jit(solution)/shard_map/all_to_all | solution.py:96
  169.8 0.7 copy.37
  170.5 10.8 %reduce-scatter.2.cloned.1.call-done = f32[16,32,128]{2,1,0:T(8,128)} async-done(((f32[16,128,128]{2,1,0:T(8,128)}), f32[16,32,128]{2,1,0:T(8,128)}) %reduce-scatter.2.cloned.1.call-update) | async-done | bytes 262160 | tf_op jit(solution)/shard_map/reduce_scatter | solution.py:142
  181.3 1.8 add_divide_fusion
  (77 shorter events, 10.4 us)
Async XLA Ops:
  7.2 134.3 %copy-start = (f32[1024,128]{1,0:T(8,128)S(1)}, f32[1024,128]{1,0:T(8,128)}, u32[]{:S(2)}) copy-start(f32[1024,128]{1,0:T(8,128)} %param.28) | copy-start | bytes 1572868
  7.2 9.9 %copy-start.11 = (f32[64]{0:T(128)S(1)}, f32[64]{0:T(128)}, u32[]{:S(2)}) copy-start(f32[64]{0:T(128)} %param.22) | copy-start | bytes 772
  7.2 9.9 %copy-start.12 = (s32[128]{0:T(128)S(1)}, s32[128]{0:T(128)}, u32[]{:S(2)}) copy-start(s32[128]{0:T(128)} %param.17) | copy-start | bytes 1540
  9.6 34.2 %copy-start.4 = (f32[256]{0:T(256)S(1)}, f32[256]{0:T(256)}, u32[]{:S(2)}) copy-start(f32[256]{0:T(256)} %param.20) | copy-start | bytes 3076
  9.6 34.2 %copy-start.5 = (f32[256]{0:T(256)S(1)}, f32[256]{0:T(256)}, u32[]{:S(2)}) copy-start(f32[256]{0:T(256)} %param.19) | copy-start | bytes 3076
  9.6 33.2 %all-to-all-start = ((bf16[16,8,16,256]{3,2,0,1:T(8,128)(2,1)}), bf16[16,8,16,256]{3,2,0,1:T(8,128)(2,1)S(1)}, u32[]{:S(2)}, u32[]{:S(2)}) async-start(bf16[16,8,16,256]{3,2,0,1:T(8,128)(2,1)} %copy.34), calls=%async_computation | async-start | bytes 2097152 | tf_op jit(solution)/shard_map/all_to_all | solution.py:58
  17.0 77.9 %all-reduce.2.cloned.1.call-start = ((), (), s32[]{:S(2)}) async-start(), calls=%async_computation.3 | async-start | bytes 2097152 | tf_op jit(solution)/shard_map/psum | solution.py:92
  43.8 1.1 copy-start.1
  56.4 1.5 copy-start.2
  57.3 3.6 %copy-start.10 = (s32[128]{0:T(128)S(1)}, s32[128]{0:T(128)}, u32[]{:S(2)}) copy-start(s32[128]{0:T(128)} %param.18) | copy-start | bytes 1540
  57.3 37.5 %copy-start.6 = (f32[256]{0:T(256)S(1)}, f32[256]{0:T(256)}, u32[]{:S(2)}) copy-start(f32[256]{0:T(256)} %param.24) | copy-start | bytes 3076
  57.8 40.0 %copy-start.7 = (f32[256]{0:T(256)S(1)}, f32[256]{0:T(256)}, u32[]{:S(2)}) copy-start(f32[256]{0:T(256)} %param.26) | copy-start | bytes 3076
  57.9 40.0 %copy-start.8 = (f32[256]{0:T(256)S(1)}, f32[256]{0:T(256)}, u32[]{:S(2)}) copy-start(f32[256]{0:T(256)} %param.25) | copy-start | bytes 3076
  57.9 41.2 %copy-start.3 = (bf16[256,2,32]{0,2,1:T(8,128)(2,1)S(1)}, bf16[256,2,32]{0,2,1:T(8,128)(2,1)}, u32[]{:S(2)}) copy-start(bf16[256,2,32]{0,2,1:T(8,128)(2,1)} %param.27) | copy-start | bytes 98308
  59.3 121.9 %reduce-scatter.2.cloned.1.call-start = ((), (), s32[]{:S(2)}) async-start(), calls=%async_computation.4 | async-start | bytes 1310720 | tf_op jit(solution)/shard_map/reduce_scatter | solution.py:142
  156.3 24.9 %copy-start.9 = (f32[128]{0:T(128)S(1)}, f32[128]{0:T(128)}, u32[]{:S(2)}) copy-start(f32[128]{0:T(128)} %param.29) | copy-start | bytes 1540
  156.4 13.4 %all-to-all-start.1 = ((bf16[32,16,256]{2,1,0:T(8,128)(2,1)}), bf16[32,16,256]{2,1,0:T(8,128)(2,1)S(1)}, u32[]{:S(2)}, u32[]{:S(2)}) async-start(bf16[32,16,256]{2,1,0:T(8,128)(2,1)} %bitcast.29), calls=%async_computation.1 | async-start | bytes 524288 | tf_op jit(solution)/shard_map/all_to_all | solution.py:96
Sparse Core Ops, SparseCore 0:
  59.5 35.3 all-reduce.1
  156.5 24.7 reduce-scatter.1
